TPU v7x, 128 devices: a whole 4x4x4 slice. The times are simulated.
128 devices in a mesh: row: 16 (over z, y_hi, core), col: 8 (over y_lo, x).
Axes of the slice: x: 4, y: 4 (y_hi: 2, y_lo: 2; y = y_hi * 2 + y_lo), z: 4, core: 2. Of those that a mesh axis runs over, the one named last changes fastest.
Arguments:
- sky_image: bfloat16 [2, 16384, 16384], P(None, 'row', 'col'), may hold values from -6 to 6
- facet_rows: int32 [128], replicated, may hold values from 512 to 15872
- facet_offsets: int32 [128], replicated, may hold values from 0 to 127
- facet_owner: int32 [128], replicated, may hold values from 0 to 127, each once
Outputs:
- facets: bfloat16 [128, 2, 1024, 1024], P(('row', 'col'))
Inputs may be any that keep to these rules, and one draw needn't show every extreme that they name: `facet_owner`: the entries are distinct, so every device owns exactly one facet.
All inputs are finite; a program needn't handle non-finite values.
Results may differ from a plain program's by a relative error of at most 0.0095.
Values may be sent and summed in bfloat16 or wider, within the bound.
No kernel may reach another device: no remote copies, remote signals or barrier semaphores. Data moves between devices by JAX's collectives and lax.ppermute only.
A program may use at most 128 MiB of HBM per device.

v0:
```python
import math
from functools import partial

import jax
import jax.numpy as jnp
import numpy as np
from jax import lax
from jax.experimental import pallas as pl
from jax.experimental.pallas import tpu as pltpu
from jax.sharding import PartitionSpec as P

N = 16384
FS = 1024
L = 128
REACH = 4
MIB = 1 << 20
PITCH = 2 * L + 4
ROW_GROUPS = 2


def dft_parts():
    k = np.arange(L)
    angles = (k[:, None] * k[None, :] % L) * (-2.0 * math.pi / L)
    scale = 1.0 / math.sqrt(L)
    return np.cos(angles) * scale, np.sin(angles) * scale


def twiddles():
    k = np.arange(L)
    angles = (k[:, None] * k[None, :] % N) * (-2.0 * math.pi / N)
    return np.stack((np.cos(angles), np.sin(angles))).astype(np.float32)


def real_form(order):
    re, im = dft_parts()
    plane = np.array([o[0] for o in order])
    index = np.array([o[1] for o in order])
    top = np.where(plane[None, :] == 0, re[:, index], -im[:, index])
    low = np.where(plane[None, :] == 0, im[:, index], re[:, index])
    return jnp.asarray(np.concatenate((top, low)), jnp.bfloat16)


def in_hbm(array):
    return pltpu.with_memory_space_constraint(array, pltpu.HBM)


def params(limit):
    return pltpu.CompilerParams(vmem_limit_bytes=limit * MIB)


PACK_ROWS = 64
AHEAD = 4


def pack_body(x_ref, out_ref, taken, given, scr, in_sems, out_sems):
    slices = x_ref.shape[1] // PACK_ROWS

    def fetch(k):
        return pltpu.make_async_copy(x_ref.at[:, pl.ds(k * PACK_ROWS, PACK_ROWS), :], taken.at[k], in_sems.at[k])

    def store(k):
        return pltpu.make_async_copy(given.at[k], out_ref.at[pl.ds(k * PACK_ROWS, PACK_ROWS)], out_sems.at[k])

    for k in range(AHEAD):
        fetch(k).start()

    def one(k, carry):
        fetch(k).wait()

        @pl.when(k + AHEAD < slices)
        def _():
            fetch(k + AHEAD).start()

        for plane in range(2):
            for a in range(16):
                scr[pl.ds((plane * 16 + a) * 68, PACK_ROWS), :] = taken[k, plane, :, a * L : (a + 1) * L].astype(
                    jnp.float32
                )
            for i in range(PACK_ROWS):
                given[k, i, plane] = scr[pl.ds(plane * 16 * 68 + i, 16, stride=68), :].astype(jnp.bfloat16)
        store(k).start()
        return carry

    lax.fori_loop(0, slices, one, 0)

    def drain(k, carry):
        store(k).wait()
        return carry

    lax.fori_loop(0, slices, drain, 0)


def pack(image):
    rows = image.shape[1]
    slices = rows // PACK_ROWS
    return pl.pallas_call(
        pack_body,
        name="pack",
        in_specs=[pl.BlockSpec(memory_space=pl.ANY)],
        out_specs=pl.BlockSpec(memory_space=pl.ANY),
        out_shape=pltpu.HBM((rows, 2, 16, L), jnp.bfloat16),
        scratch_shapes=[
            pltpu.VMEM((slices, 2, PACK_ROWS, 16 * L), jnp.bfloat16),
            pltpu.VMEM((slices, PACK_ROWS, 2, 16, L), jnp.bfloat16),
            pltpu.VMEM((2 * 16 * 68, L), jnp.float32),
            pltpu.SemaphoreType.DMA((slices,)),
            pltpu.SemaphoreType.DMA((slices,)),
        ],
        compiler_params=params(32),
    )(in_hbm(image))


def rows_body(x_ref, g_ref, h_ref, tw_ref, out_ref, scr):
    first = pl.program_id(0) * 16 * ROW_GROUPS
    for group in range(ROW_GROUPS):
        base = group * 16 * PITCH
        row = pl.multiple_of(first + group * 16, 16)
        for pair in range(8):
            data = jnp.concatenate([x_ref[:, row + 2 * pair + e].reshape(2 * L, L) for e in range(2)], axis=1)
            mixed = jnp.dot(g_ref[...], data, preferred_element_type=jnp.float32)
            turned = []
            for e in range(2):
                re = mixed[:L, e * L : (e + 1) * L]
                im = mixed[L:, e * L : (e + 1) * L]
                turned.append(
                    jnp.concatenate(
                        (
                            (re * tw_ref[0] - im * tw_ref[1]).astype(jnp.bfloat16),
                            (re * tw_ref[1] + im * tw_ref[0]).astype(jnp.bfloat16),
                        ),
                        axis=1,
                    )
                )
            section = jnp.concatenate(turned, axis=0)
            done = lax.dot_general(h_ref[...], section, (((1,), (1,)), ((), ())), preferred_element_type=jnp.float32)
            for e in range(2):
                scr[pl.ds(base + (2 * pair + e) * PITCH, 2 * L), :] = done[:, e * L : (e + 1) * L]
        for plane in range(2):
            for q in range(L):
                tile = scr[pl.ds(base + plane * L + q, 16, stride=PITCH), :]
                out_ref[q, plane, pl.ds(row, 16), :] = tile.astype(jnp.bfloat16)


def rows_pass(x, g, h, tw):
    _, rows = x.shape[:2]
    whole = lambda j: (0, 0)
    return pl.pallas_call(
        rows_body,
        name="rows_pass",
        grid=(rows // (16 * ROW_GROUPS),),
        in_specs=[
            pl.BlockSpec(memory_space=pltpu.VMEM),
            pl.BlockSpec((2 * L, 2 * L), whole),
            pl.BlockSpec((2 * L, 2 * L), whole),
            pl.BlockSpec((2, L, L), lambda j: (0, 0, 0)),
        ],
        out_specs=pl.BlockSpec(memory_space=pltpu.VMEM),
        out_shape=jax.ShapeDtypeStruct((L, 2, rows, L), jnp.bfloat16),
        scratch_shapes=[pltpu.VMEM((ROW_GROUPS * 16 * PITCH, L), jnp.float32)],
        compiler_params=params(24),
    )(x, g, h, tw)


STEPS = 4
BANDS = 4


def columns_body(starts_ref, x_ref, g_ref, tw_ref, f_ref, *refs):
    outs = refs[:-6]
    spreads, turns = refs[-6:-4], refs[-4:-2]
    section, grid = refs[-2:]
    step = pl.program_id(0)
    per = L // BANDS

    @pl.when(step < STEPS)
    def _():
        for group, (spread, turned) in enumerate(zip(spreads, turns)):
            rows = pl.ds(pl.multiple_of(step * 32 + group * 16, 16), 16)
            for k in range(2 * L):
                tile = x_ref[k // 2, k % 2, group * 16 : group * 16 + 16]
                spread[pl.ds(k * 20, 16), :] = tile.astype(jnp.float32)
            for pair in range(8):
                data = jnp.concatenate(
                    [spread[pl.ds(2 * pair + e, 2 * L, stride=20), :].astype(jnp.bfloat16) for e in range(2)], axis=1
                )
                mixed = jnp.dot(g_ref[...], data, preferred_element_type=jnp.float32)
                for e in range(2):
                    i = 2 * pair + e
                    re = mixed[:L, e * L : (e + 1) * L]
                    im = mixed[L:, e * L : (e + 1) * L]
                    at = group * 16 + i
                    t_re = jnp.broadcast_to(tw_ref[0, 0, :, at : at + 1], (L, L))
                    t_im = jnp.broadcast_to(tw_ref[0, 1, :, at : at + 1], (L, L))
                    turned[pl.ds(i * PITCH, L), :] = re * t_re - im * t_im
                    turned[pl.ds(i * PITCH + L, L), :] = re * t_im + im * t_re
            for plane in range(2):
                for p in range(L):
                    tile = turned[pl.ds(plane * L + p, 16, stride=PITCH), :]
                    section[p, plane, rows, :] = tile.astype(jnp.bfloat16)

    @pl.when(step == STEPS)
    def _():
        def second(k, carry):
            for pair in range(per // 2):
                p = k * per + 2 * pair
                data = jnp.concatenate([section[p + e].reshape(2 * L, L) for e in range(2)], axis=1)
                done = jnp.dot(f_ref[...], data, preferred_element_type=jnp.float32)
                for e in range(2):
                    grid[pl.ds((p + e) * PITCH, 2 * L), :] = done[:, e * L : (e + 1) * L]
            return carry

        lax.fori_loop(0, BANDS, second, 0)
        for p in range(16):
            grid[pl.ds((L + p) * PITCH, 2 * L), :] = grid[pl.ds(p * PITCH + 1, 2 * L), :]
        for slot, out_ref in enumerate(outs):
            start = starts_ref[slot]
            top = start // L
            shift = start % L
            for group in range(L // 16):
                p = shift + 16 * group
                wrapped = (p >= L).astype(jnp.int32)
                base = (p - L * wrapped) * PITCH + top + wrapped
                for plane in range(2):
                    for u in range(FS // L):
                        tile = grid[pl.ds(base + plane * L + u, 16, stride=PITCH), :]
                        out_ref[plane, u * L + 16 * group : u * L + 16 * group + 16, :] = tile.astype(jnp.bfloat16)


def columns_pass(x, g, tw, f, starts):
    targets = starts.shape[0]
    whole = lambda j, s: (0, 0)
    return pl.pallas_call(
        columns_body,
        name="columns_pass",
        grid_spec=pltpu.PrefetchScalarGridSpec(
            num_scalar_prefetch=1,
            grid=(STEPS + 1,),
            in_specs=[
                pl.BlockSpec((L, 2, 32, L), lambda j, s: (0, 0, jnp.minimum(j, STEPS - 1), 0)),
                pl.BlockSpec((2 * L, 2 * L), whole),
                pl.BlockSpec((1, 2, L, 32), lambda j, s: (jnp.minimum(j, STEPS - 1), 0, 0, 0)),
                pl.BlockSpec((2 * L, 2 * L), whole),
            ],
            out_specs=[pl.BlockSpec(memory_space=pltpu.VMEM)] * targets,
            scratch_shapes=[pltpu.VMEM((2 * L * 20, L), jnp.float32)] * 2
            + [pltpu.VMEM((16 * PITCH, L), jnp.float32)] * 2
            + [
                pltpu.VMEM((L, 2, L, L), jnp.bfloat16),
                pltpu.VMEM(((L + 16) * PITCH, L), jnp.float32),
            ],
        ),
        out_shape=[jax.ShapeDtypeStruct((2, FS, L), jnp.bfloat16)] * targets,
        compiler_params=params(46),
    )(starts, in_hbm(x), g, tw, f)


def facet_body_at(half, scal_ref, *refs):
    strips, down_ref, across_ref = refs[: REACH + 1], refs[REACH + 1], refs[REACH + 2]
    out_ref, ready, sems = refs[-3:]
    shift = scal_ref[0]
    owned = scal_ref[1].astype(jnp.float32)
    keep = lax.broadcasted_iota(jnp.int32, (16, L), 1) < L - shift
    back = lax.rem(L - shift, L)
    width = REACH * L
    block = L

    def store(k):
        rows = pl.ds(k * block, block)
        target = out_ref.at[0, :, rows, pl.ds(half * width, width)]
        return pltpu.make_async_copy(ready.at[:, rows, :], target, sems.at[k])

    def one(k, carry):
        for r in range(0, block, 16):
            rows = pl.ds(pl.multiple_of(k * block + r, 16), 16)
            down = jnp.broadcast_to(down_ref[rows], (16, L)) * owned
            for plane in range(2):
                last = pltpu.roll(strips[0][plane, rows].astype(jnp.float32), back, 1)
                for j in range(REACH):
                    this = pltpu.roll(strips[j + 1][plane, rows].astype(jnp.float32), back, 1)
                    weight = down * across_ref[:, j * L : (j + 1) * L]
                    tile = jnp.where(keep, last, this) * weight
                    ready[plane, rows, j * L : (j + 1) * L] = tile.astype(jnp.bfloat16)
                    last = this
        store(k).start()
        return carry

    lax.fori_loop(0, FS // block, one, 0)
    for k in range(FS // block):
        store(k).wait()


def facet_half(half, strips, scalars, before):
    taper = (0.25 + 0.75 * np.sin(math.pi * (np.arange(FS) + 0.5) / FS)).astype(np.float32)
    width = REACH * L
    vmem = pl.BlockSpec(memory_space=pltpu.VMEM)
    anywhere = pl.BlockSpec(memory_space=pl.ANY)
    args = [*strips, jnp.asarray(taper[:, None]), jnp.asarray(taper[None, half * width : (half + 1) * width])]
    extra = {}
    if before is not None:
        extra = dict(input_output_aliases={len(args) + 1: 0})
        args.append(before)
    return pl.pallas_call(
        partial(facet_body_at, half),
        name="facet",
        in_specs=[pl.BlockSpec(memory_space=pltpu.SMEM)]
        + [vmem] * (len(strips) + 2)
        + [anywhere] * (len(args) - len(strips) - 2),
        out_specs=anywhere,
        out_shape=pltpu.HBM((1, 2, FS, FS), jnp.bfloat16),
        scratch_shapes=[pltpu.VMEM((2, FS, width), jnp.bfloat16), pltpu.SemaphoreType.DMA((FS // L,))],
        compiler_params=params(16),
        **extra,
    )(scalars, *args)


def shifted(block, axis, distance):
    devices = range(lax.axis_size(axis))
    route = [((i - distance) % len(devices), i) for i in devices]
    return lax.ppermute(block, axis, route)


def shards(sky_image, facet_rows, facet_offsets, facet_owner):
    both = ("row", "col")
    devices = lax.axis_size(both)
    first_rows = real_form([(plane, 16 * c + a) for c in range(8) for plane in range(2) for a in range(16)])
    second_rows = real_form([(plane, b) for plane in range(2) for b in range(L)])
    first_cols = real_form([(plane, s) for s in range(L) for plane in range(2)])
    second_cols = real_form([(plane, i) for plane in range(2) for i in range(L)])
    turn = twiddles()
    turn_cols = turn.reshape(2, L, STEPS, L // STEPS).transpose(2, 0, 1, 3)

    my_index = lax.axis_index(both)
    targets = (my_index + jnp.arange(REACH, -REACH - 1, -1, dtype=jnp.int32)) % devices
    matches = (facet_owner[None, :] == targets[:, None]).astype(jnp.int32)
    owned = jnp.sum(matches, axis=1)
    starts = jnp.where(owned > 0, jnp.sum(matches * facet_rows[None, :], axis=1) - FS // 2, 0)
    offset = jnp.sum(matches[REACH] * facet_offsets)
    scalars = jnp.stack((offset, owned[REACH]))

    sent = pack(sky_image)
    sent, starts, scalars = lax.optimization_barrier((sent, starts, scalars))
    strip = lax.all_to_all(sent, "col", split_axis=0, concat_axis=0, tiled=True)
    strip = strip.reshape(lax.axis_size("col"), L, 2, 16, L)
    done = rows_pass(strip, first_rows, second_rows, jnp.asarray(turn))
    columns = lax.all_to_all(done, both, split_axis=0, concat_axis=0, tiled=True)
    cut = columns_pass(columns, first_cols, jnp.asarray(turn_cols), second_cols, starts)
    strips = []
    for slot, distance in enumerate(range(REACH, -REACH - 1, -1)):
        strips.append(cut[slot] if distance == 0 else shifted(cut[slot], both, distance))
    facets = facet_half(0, strips[: REACH + 1], scalars, None)
    return facet_half(1, strips[REACH:], scalars, facets)


def solution(mesh):
    placed = (P(None, "row", "col"), P(), P(), P())
    return jax.shard_map(
        shards,
        mesh=mesh,
        in_specs=placed,
        out_specs=P(("row", "col"), None, None, None),
        check_vma=False,
    )
```

profile of v0, /device:TPU:21, one launch (start us, length us, event | category | flops | bytes accessed | tf_op | source)
XLA Modules:
  0.0 323.6 jit_solution(4786701001746812165)
XLA Ops:
  0.0 0.7 compare_convert_fusion
  0.7 0.9 fusion
  1.6 0.6 slice.7
  2.2 7.4 %pack.1 = bf16[1024,2,16,128]{3,2,1,0:T(8,128)(2,1)} custom-call(bf16[2,1024,2048]{2,1,0:T(8,128)(2,1)} %x_ref.1), custom_call_target="tpu_custom_call" | custom-call | tf_op jit(solution)/shard_map/pack/pallas_call | solution.py:96
  9.6 0.0 copy-done.8
  9.6 0.7 fusion.4
  10.3 1.3 pad_add_fusion.scal_ref
  11.7 96.8 %all_to_all.10 = bf16[1024,2,16,128]{3,2,1,0:T(8,128)(2,1)S(1)} all-to-all(bf16[1024,2,16,128]{3,2,1,0:T(8,128)(2,1)} %pack.1), channel_id=1, replica_groups=mesh['row'=16,'col'=8] {'col'}, dimensions={0} | all-to-all | bytes 16777216 | tf_op jit(solution)/shard_map/all_to_all | solution.py:342
  108.4 7.1 %rows_pass.1 = bf16[128,2,128,128]{3,2,1,0:T(8,128)(2,1)S(1)} custom-call(bf16[8,128,2,16,128]{4,3,2,1,0:T(8,128)(2,1)S(1)} %bitcast.8, bf16[256,256]{1,0:T(8,128)(2,1)S(1)} %copy-done.5, bf16[256,256]{1,0:T(8,128)(2,1)S(1)} %copy-done.1, f32[2,128,128]{2,1,0:T(8,128)S(1)} %copy-done.4), custom_call_target="tpu_custom_call" | custom-call | tf_op jit(solution)/shard_map/rows_pass/pallas_call | solution.py:147
  115.6 0.0 copy-start.2
  115.6 0.0 copy-start.3
  115.6 107.2 %all_to_all.11.x_ref = bf16[128,2,128,128]{3,2,1,0:T(8,128)(2,1)} all-to-all(bf16[128,2,128,128]{3,2,1,0:T(8,128)(2,1)S(1)} %rows_pass.1), channel_id=1, replica_groups=mesh['row'=16,'col'=8] {'row','col'}, dimensions={0} | all-to-all | bytes 16777216 | tf_op jit(solution)/shard_map/all_to_all | solution.py:345
  222.8 0.0 copy-start.6
  222.8 13.4 %columns_pass.1 = (bf16[2,1024,128]{2,1,0:T(8,128)(2,1)S(1)}, bf16[2,1024,128]{2,1,0:T(8,128)(2,1)S(1)}, bf16[2,1024,128]{2,1,0:T(8,128)(2,1)S(1)}, bf16[2,1024,...) custom-call(s32[9]{0:T(128)S(1)} %compare_select_fusion.3.starts_ref, ...), custom_call_target="tpu_custom_call" | custom-call | tf_op jit(solution)/shard_map/columns_pass/pallas_call | solution.py:232
  236.3 1.9 collective-permute-start.4
  238.2 2.9 collective-permute-start.5
  241.1 2.5 collective-permute-start.6
  243.6 0.0 collective-permute-start
  243.6 1.5 collective-permute-start.7
  245.1 15.5 %collective-permute-done.4.refs_0_ = bf16[2,1024,128]{2,1,0:T(8,128)(2,1)S(1)} collective-permute-done((bf16[2,1024,128]{2,1,0:T(8,128)(2,1)S(1)}, bf16[2,1024,128]{2,1,0:T(8,128)(2,1)S(1)}, u32[]{:S(2)}, u32[]{:S(2)}) %collective-permute-start.4) | collective-permute-done | bytes 524320 | tf_op jit(solution)/shard_map/ppermute | solution.py:319
  260.6 23.5 %collective-permute-start.1 = (bf16[2,1024,128]{2,1,0:T(8,128)(2,1)S(1)}, bf16[2,1024,128]{2,1,0:T(8,128)(2,1)S(1)}, u32[]{:S(2)}, u32[]{:S(2)}) collective-permute-start(bf16[2,1024,128]{2,1,0:T(8,128)(2,1)S(1)} %get-tuple-element.22), channel_id=1, source_target_pairs={{2,0},{3,1},{4,2},{5,3},{6,4},{7,5},{8,6},{9,7},{10,8},{11,9},{12,... | collective-permute-start | bytes 1572872 | tf_op jit(solution)/shard_map/ppermute | solution.py:319
  284.1 0.0 collective-permute-done.5.refs_1_
  284.1 0.0 collective-permute-start.2
  284.1 0.0 collective-permute-done.6.refs_2_
  284.1 4.0 %collective-permute-start.3 = (bf16[2,1024,128]{2,1,0:T(8,128)(2,1)S(1)}, bf16[2,1024,128]{2,1,0:T(8,128)(2,1)S(1)}, u32[]{:S(2)}, u32[]{:S(2)}) collective-permute-start(bf16[2,1024,128]{2,1,0:T(8,128)(2,1)S(1)} %get-tuple-element.24), channel_id=1, source_target_pairs={{4,0},{5,1},{6,2},{7,3},{8,4},{9,5},{10,6},{11,7},{12,8},{13,9},{1... | collective-permute-start | bytes 1572872 | tf_op jit(solution)/shard_map/ppermute | solution.py:319
  288.1 0.0 collective-permute-done.7.refs_3_
  288.1 2.7 facet.2.refs_7_
  290.9 0.0 collective-permute-done.refs_1_
  290.9 6.2 %collective-permute-done.1.refs_2_ = bf16[2,1024,128]{2,1,0:T(8,128)(2,1)S(1)} collective-permute-done((bf16[2,1024,128]{2,1,0:T(8,128)(2,1)S(1)}, bf16[2,1024,128]{2,1,0:T(8,128)(2,1)S(1)}, u32[]{:S(2)}, u32[]{:S(2)}) %collective-permute-start.1) | collective-permute-done | bytes 524320 | tf_op jit(solution)/shard_map/ppermute | solution.py:319
  297.1 12.5 %collective-permute-done.2.refs_3_ = bf16[2,1024,128]{2,1,0:T(8,128)(2,1)S(1)} collective-permute-done((bf16[2,1024,128]{2,1,0:T(8,128)(2,1)S(1)}, bf16[2,1024,128]{2,1,0:T(8,128)(2,1)S(1)}, u32[]{:S(2)}, u32[]{:S(2)}) %collective-permute-start.2) | collective-permute-done | bytes 524320 | tf_op jit(solution)/shard_map/ppermute | solution.py:319
  309.6 11.2 %collective-permute-done.3.refs_4_ = bf16[2,1024,128]{2,1,0:T(8,128)(2,1)S(1)} collective-permute-done((bf16[2,1024,128]{2,1,0:T(8,128)(2,1)S(1)}, bf16[2,1024,128]{2,1,0:T(8,128)(2,1)S(1)}, u32[]{:S(2)}, u32[]{:S(2)}) %collective-permute-start.3) | collective-permute-done | bytes 524320 | tf_op jit(solution)/shard_map/ppermute | solution.py:319
  320.9 2.7 facet.3
  (16 shorter events, 0.0 us)
Async XLA Ops:
  2.2 7.5 %copy-start.8 = (s32[128]{0:T(128)S(1)}, s32[128]{0:T(128)}, u32[]{:S(2)}) copy-start(s32[128]{0:T(128)} %param.16) | copy-start | bytes 1540
  11.7 96.8 %copy-start.1 = (bf16[256,256]{1,0:T(8,128)(2,1)S(1)}, bf16[256,256]{1,0:T(8,128)(2,1)}, u32[]{:S(2)}) copy-start(bf16[256,256]{1,0:T(8,128)(2,1)} %constant.53.clone.h_ref.f_ref) | copy-start | bytes 393220
  11.7 96.8 %copy-start.4 = (f32[2,128,128]{2,1,0:T(8,128)S(1)}, f32[2,128,128]{2,1,0:T(8,128)}, u32[]{:S(2)}) copy-start(f32[2,128,128]{2,1,0:T(8,128)} %constant.55.clone.tw_ref) | copy-start | bytes 393220
  11.7 96.8 %copy-start.5 = (bf16[256,256]{1,0:T(8,128)(2,1)S(1)}, bf16[256,256]{1,0:T(8,128)(2,1)}, u32[]{:S(2)}) copy-start(bf16[256,256]{1,0:T(8,128)(2,1)} %constant.52.clone.g_ref) | copy-start | bytes 393220
  115.6 107.2 %copy-start.2 = (f32[4,2,128,32]{3,2,1,0:T(8,128)S(1)}, f32[4,2,128,32]{3,2,1,0:T(8,128)}, u32[]{:S(2)}) copy-start(f32[4,2,128,32]{3,2,1,0:T(8,128)} %constant.56.clone.tw_ref) | copy-start | bytes 393220
  115.6 107.2 %copy-start.3 = (bf16[256,256]{1,0:T(8,128)(2,1)S(1)}, bf16[256,256]{1,0:T(8,128)(2,1)}, u32[]{:S(2)}) copy-start(bf16[256,256]{1,0:T(8,128)(2,1)} %constant.54.clone.g_ref) | copy-start | bytes 393220
  222.8 65.3 %copy-start = (f32[1024,1]{1,0:T(8,128)S(1)}, f32[1024,1]{1,0:T(8,128)}, u32[]{:S(2)}) copy-start(f32[1024,1]{1,0:T(8,128)} %constant.57.clone.refs_5_) | copy-start | bytes 12292
  222.8 65.3 %copy-start.7 = (f32[1,512]{1,0:T(1,128)S(1)}, f32[1,512]{1,0:T(1,128)}, u32[]{:S(2)}) copy-start(f32[1,512]{1,0:T(1,128)} %constant.58.clone.refs_6_) | copy-start | bytes 6148
  222.8 98.0 %copy-start.6 = (f32[1,512]{1,0:T(1,128)S(1)}, f32[1,512]{1,0:T(1,128)}, u32[]{:S(2)}) copy-start(f32[1,512]{1,0:T(1,128)} %constant.59.clone.refs_6_) | copy-start | bytes 6148
  236.3 24.3 %collective-permute-start.4 = (bf16[2,1024,128]{2,1,0:T(8,128)(2,1)S(1)}, bf16[2,1024,128]{2,1,0:T(8,128)(2,1)S(1)}, u32[]{:S(2)}, u32[]{:S(2)}) collective-permute-start(bf16[2,1024,128]{2,1,0:T(8,128)(2,1)S(1)} %get-tuple-element.25), channel_id=1, source_target_pairs={{124,0},{125,1},{126,2},{127,3},{0,4},{1,5},{2,6},{3,7},{4,8},{5,9... | collective-permute-start | bytes 1572872 | tf_op jit(solution)/shard_map/ppermute | solution.py:319
  238.2 45.9 %collective-permute-start.5 = (bf16[2,1024,128]{2,1,0:T(8,128)(2,1)S(1)}, bf16[2,1024,128]{2,1,0:T(8,128)(2,1)S(1)}, u32[]{:S(2)}, u32[]{:S(2)}) collective-permute-start(bf16[2,1024,128]{2,1,0:T(8,128)(2,1)S(1)} %get-tuple-element.26), channel_id=1, source_target_pairs={{125,0},{126,1},{127,2},{0,3},{1,4},{2,5},{3,6},{4,7},{5,8},{6,9},... | collective-permute-start | bytes 1572872 | tf_op jit(solution)/shard_map/ppermute | solution.py:319
  241.1 43.0 %collective-permute-start.6 = (bf16[2,1024,128]{2,1,0:T(8,128)(2,1)S(1)}, bf16[2,1024,128]{2,1,0:T(8,128)(2,1)S(1)}, u32[]{:S(2)}, u32[]{:S(2)}) collective-permute-start(bf16[2,1024,128]{2,1,0:T(8,128)(2,1)S(1)} %get-tuple-element.27), channel_id=1, source_target_pairs={{126,0},{127,1},{0,2},{1,3},{2,4},{3,5},{4,6},{5,7},{6,8},{7,9},{8... | collective-permute-start | bytes 1572872 | tf_op jit(solution)/shard_map/ppermute | solution.py:319
  243.6 47.3 %collective-permute-start = (bf16[2,1024,128]{2,1,0:T(8,128)(2,1)S(1)}, bf16[2,1024,128]{2,1,0:T(8,128)(2,1)S(1)}, u32[]{:S(2)}, u32[]{:S(2)}) collective-permute-start(bf16[2,1024,128]{2,1,0:T(8,128)(2,1)S(1)} %get-tuple-element.21), channel_id=1, source_target_pairs={{1,0},{2,1},{3,2},{4,3},{5,4},{6,5},{7,6},{8,7},{9,8},{10,9},{11,1... | collective-permute-start | bytes 1572872 | tf_op jit(solution)/shard_map/ppermute | solution.py:319
  243.6 44.5 %collective-permute-start.7 = (bf16[2,1024,128]{2,1,0:T(8,128)(2,1)S(1)}, bf16[2,1024,128]{2,1,0:T(8,128)(2,1)S(1)}, u32[]{:S(2)}, u32[]{:S(2)}) collective-permute-start(bf16[2,1024,128]{2,1,0:T(8,128)(2,1)S(1)} %get-tuple-element.28), channel_id=1, source_target_pairs={{127,0},{0,1},{1,2},{2,3},{3,4},{4,5},{5,6},{6,7},{7,8},{8,9},{9,1... | collective-permute-start | bytes 1572872 | tf_op jit(solution)/shard_map/ppermute | solution.py:319
  260.6 36.5 %collective-permute-start.1 = (bf16[2,1024,128]{2,1,0:T(8,128)(2,1)S(1)}, bf16[2,1024,128]{2,1,0:T(8,128)(2,1)S(1)}, u32[]{:S(2)}, u32[]{:S(2)}) collective-permute-start(bf16[2,1024,128]{2,1,0:T(8,128)(2,1)S(1)} %get-tuple-element.22), channel_id=1, source_target_pairs={{2,0},{3,1},{4,2},{5,3},{6,4},{7,5},{8,6},{9,7},{10,8},{11,9},{12,... | collective-permute-start | bytes 1572872 | tf_op jit(solution)/shard_map/ppermute | solution.py:319
  284.1 25.5 %collective-permute-start.2 = (bf16[2,1024,128]{2,1,0:T(8,128)(2,1)S(1)}, bf16[2,1024,128]{2,1,0:T(8,128)(2,1)S(1)}, u32[]{:S(2)}, u32[]{:S(2)}) collective-permute-start(bf16[2,1024,128]{2,1,0:T(8,128)(2,1)S(1)} %get-tuple-element.23), channel_id=1, source_target_pairs={{3,0},{4,1},{5,2},{6,3},{7,4},{8,5},{9,6},{10,7},{11,8},{12,9},{13... | collective-permute-start | bytes 1572872 | tf_op jit(solution)/shard_map/ppermute | solution.py:319
  284.1 36.8 %collective-permute-start.3 = (bf16[2,1024,128]{2,1,0:T(8,128)(2,1)S(1)}, bf16[2,1024,128]{2,1,0:T(8,128)(2,1)S(1)}, u32[]{:S(2)}, u32[]{:S(2)}) collective-permute-start(bf16[2,1024,128]{2,1,0:T(8,128)(2,1)S(1)} %get-tuple-element.24), channel_id=1, source_target_pairs={{4,0},{5,1},{6,2},{7,3},{8,4},{9,5},{10,6},{11,7},{12,8},{13,9},{1... | collective-permute-start | bytes 1572872 | tf_op jit(solution)/shard_map/ppermute | solution.py:319
where the time goes:
time: 324 us
  blocking collectives  204 us (63%)
  waiting for transfers between devices  45.5 us (14%)
  starting transfers between devices  36.3 us (11%)
  Pallas kernels  33.5 us (10%)
  other arithmetic  3.62 us (1%)
    all_to_all x1, blocking collectives, shards(): lax.all_to_all(done, both, split_axis=0, concat_axis=0, tiled=True)  107 us
    all_to_all x1, blocking collectives, shards(): strip = lax.all_to_all(sent, 'col', split_axis=0, concat_axis=0, tiled=True)  96.8 us
    ppermute x8, waiting for transfers between devices, shifted(): return lax.ppermute(block, axis, route)  45.5 us
    ppermute x8, starting transfers between devices, shifted(): return lax.ppermute(block, axis, route)  36.3 us
    pallas_call x1, Pallas kernels, columns_pass(): pl.pallas_call(columns_body, name='columns_pass', grid_spec=pltpu.Prefetc...  13.4 us
    pallas_call x1, Pallas kernels, pack(): pl.pallas_call(pack_body, name='pack', in_specs=[pl.BlockSpec(memory_spac...  7.44 us
    pallas_call x1, Pallas kernels, rows_pass(): pl.pallas_call(rows_body, name='rows_pass', grid=(rows // (16 * ROW_GROUP...  7.13 us
  transfers between devices with their start and end apart: 8, of which 4 were waited for; matrix products, arithmetic and copies ran while one was open for 0% of the time, Pallas kernels for 1%

commit v1 on v0

--- a/solution.py
+++ b/solution.py
@@ -50,9 +50,11 @@
 
 PACK_ROWS = 64
 AHEAD = 4
-
-
-def pack_body(x_ref, out_ref, taken, given, scr, in_sems, out_sems):
+OFFSET = 2 * REACH + 1
+OWNED = 2 * REACH + 2
+
+
+def pack_body(mine_ref, x_ref, rows_ref, offsets_ref, owner_ref, out_ref, table_ref, taken, given, scr, in_sems, out_sems, small_tables, small_sems):
     slices = x_ref.shape[1] // PACK_ROWS
 
     def fetch(k):
@@ -63,6 +65,13 @@
 
     for k in range(AHEAD):
         fetch(k).start()
+
+    def small(k, source):
+        return pltpu.make_async_copy(source, small_tables.at[k], small_sems.at[k])
+
+    sources = (rows_ref, offsets_ref, owner_ref)
+    for k, source in enumerate(sources):
+        small(k, source).start()
 
     def one(k, carry):
         fetch(k).wait()
@@ -82,6 +91,14 @@
         return carry
 
     lax.fori_loop(0, slices, one, 0)
+    for k, source in enumerate(sources):
+        small(k, source).wait()
+    slot = lax.broadcasted_iota(jnp.int32, (16, L), 0)
+    target = lax.rem(mine_ref[0] + REACH - jnp.where(slot <= 2 * REACH, slot, REACH) + L, L)
+    match = small_tables[2] == target
+    pick = jnp.where(slot <= 2 * REACH, small_tables[0] - FS // 2, jnp.where(slot == OFFSET, small_tables[1], 1))
+    chosen = jnp.sum(jnp.where(match, pick, 0).astype(jnp.float32), axis=1, keepdims=True)
+    table_ref[...] = jnp.broadcast_to(chosen, (16, L)).astype(jnp.int32)
 
     def drain(k, carry):
         store(k).wait()
@@ -90,24 +107,30 @@
     lax.fori_loop(0, slices, drain, 0)
 
 
-def pack(image):
+def pack(image, mine, facet_rows, facet_offsets, facet_owner):
     rows = image.shape[1]
     slices = rows // PACK_ROWS
+    vmem = pl.BlockSpec(memory_space=pltpu.VMEM)
     return pl.pallas_call(
         pack_body,
         name="pack",
-        in_specs=[pl.BlockSpec(memory_space=pl.ANY)],
-        out_specs=pl.BlockSpec(memory_space=pl.ANY),
-        out_shape=pltpu.HBM((rows, 2, 16, L), jnp.bfloat16),
+        in_specs=[pl.BlockSpec(memory_space=pltpu.SMEM), *[pl.BlockSpec(memory_space=pl.ANY)] * 4],
+        out_specs=[pl.BlockSpec(memory_space=pl.ANY), vmem],
+        out_shape=[
+            pltpu.HBM((rows, 2, 16, L), jnp.bfloat16),
+            jax.ShapeDtypeStruct((16, L), jnp.int32),
+        ],
         scratch_shapes=[
             pltpu.VMEM((slices, 2, PACK_ROWS, 16 * L), jnp.bfloat16),
             pltpu.VMEM((slices, PACK_ROWS, 2, 16, L), jnp.bfloat16),
             pltpu.VMEM((2 * 16 * 68, L), jnp.float32),
             pltpu.SemaphoreType.DMA((slices,)),
             pltpu.SemaphoreType.DMA((slices,)),
+            pltpu.VMEM((3, 1, L), jnp.int32),
+            pltpu.SemaphoreType.DMA((3,)),
         ],
         compiler_params=params(32),
-    )(in_hbm(image))
+    )(mine, in_hbm(image), *(in_hbm(t.reshape(1, L)) for t in (facet_rows, facet_offsets, facet_owner)))
 
 
 def rows_body(x_ref, g_ref, h_ref, tw_ref, out_ref, scr):
@@ -213,7 +236,7 @@
         for p in range(16):
             grid[pl.ds((L + p) * PITCH, 2 * L), :] = grid[pl.ds(p * PITCH + 1, 2 * L), :]
         for slot, out_ref in enumerate(outs):
-            start = starts_ref[slot]
+            start = starts_ref[slot, 0]
             top = start // L
             shift = start % L
             for group in range(L // 16):
@@ -227,7 +250,7 @@
 
 
 def columns_pass(x, g, tw, f, starts):
-    targets = starts.shape[0]
+    targets = 2 * REACH + 1
     whole = lambda j, s: (0, 0)
     return pl.pallas_call(
         columns_body,
@@ -257,8 +280,8 @@
 def facet_body_at(half, scal_ref, *refs):
     strips, down_ref, across_ref = refs[: REACH + 1], refs[REACH + 1], refs[REACH + 2]
     out_ref, ready, sems = refs[-3:]
-    shift = scal_ref[0]
-    owned = scal_ref[1].astype(jnp.float32)
+    shift = scal_ref[OFFSET, 0]
+    owned = scal_ref[OWNED, 0].astype(jnp.float32)
     keep = lax.broadcasted_iota(jnp.int32, (16, L), 1) < L - shift
     back = lax.rem(L - shift, L)
     width = REACH * L
@@ -321,7 +344,6 @@
 
 def shards(sky_image, facet_rows, facet_offsets, facet_owner):
     both = ("row", "col")
-    devices = lax.axis_size(both)
     first_rows = real_form([(plane, 16 * c + a) for c in range(8) for plane in range(2) for a in range(16)])
     second_rows = real_form([(plane, b) for plane in range(2) for b in range(L)])
     first_cols = real_form([(plane, s) for s in range(L) for plane in range(2)])
@@ -330,25 +352,17 @@
     turn_cols = turn.reshape(2, L, STEPS, L // STEPS).transpose(2, 0, 1, 3)
 
     my_index = lax.axis_index(both)
-    targets = (my_index + jnp.arange(REACH, -REACH - 1, -1, dtype=jnp.int32)) % devices
-    matches = (facet_owner[None, :] == targets[:, None]).astype(jnp.int32)
-    owned = jnp.sum(matches, axis=1)
-    starts = jnp.where(owned > 0, jnp.sum(matches * facet_rows[None, :], axis=1) - FS // 2, 0)
-    offset = jnp.sum(matches[REACH] * facet_offsets)
-    scalars = jnp.stack((offset, owned[REACH]))
-
-    sent = pack(sky_image)
-    sent, starts, scalars = lax.optimization_barrier((sent, starts, scalars))
+    sent, table = pack(sky_image, my_index.astype(jnp.int32)[None], facet_rows, facet_offsets, facet_owner)
     strip = lax.all_to_all(sent, "col", split_axis=0, concat_axis=0, tiled=True)
     strip = strip.reshape(lax.axis_size("col"), L, 2, 16, L)
     done = rows_pass(strip, first_rows, second_rows, jnp.asarray(turn))
     columns = lax.all_to_all(done, both, split_axis=0, concat_axis=0, tiled=True)
-    cut = columns_pass(columns, first_cols, jnp.asarray(turn_cols), second_cols, starts)
+    cut = columns_pass(columns, first_cols, jnp.asarray(turn_cols), second_cols, table)
     strips = []
     for slot, distance in enumerate(range(REACH, -REACH - 1, -1)):
         strips.append(cut[slot] if distance == 0 else shifted(cut[slot], both, distance))
-    facets = facet_half(0, strips[: REACH + 1], scalars, None)
-    return facet_half(1, strips[REACH:], scalars, facets)
+    facets = facet_half(0, strips[: REACH + 1], table, None)
+    return facet_half(1, strips[REACH:], table, facets)
 
 
 def solution(mesh):

time: 324 us -> 320 us (0.988)
  other arithmetic: 3.62 us -> 0 us
where the time goes in v1:
time: 320 us
  blocking collectives  204 us (64%)
  waiting for transfers between devices  45.4 us (14%)
  starting transfers between devices  36.3 us (11%)
  Pallas kernels  34.2 us (11%)
    all_to_all x1, blocking collectives, shards(): lax.all_to_all(done, both, split_axis=0, concat_axis=0, tiled=True)  107 us
    all_to_all x1, blocking collectives, shards(): strip = lax.all_to_all(sent, 'col', split_axis=0, concat_axis=0, tiled=True)  96.8 us
    ppermute x8, waiting for transfers between devices, shifted(): return lax.ppermute(block, axis, route)  45.4 us
    ppermute x8, starting transfers between devices, shifted(): return lax.ppermute(block, axis, route)  36.3 us
    pallas_call x1, Pallas kernels, columns_pass(): pl.pallas_call(columns_body, name='columns_pass', grid_spec=pltpu.Prefetc...  13.8 us
    pallas_call x1, Pallas kernels, pack(): pl.pallas_call(pack_body, name='pack', in_specs=[pl.BlockSpec(memory_spac...  7.44 us
    pallas_call x1, Pallas kernels, rows_pass(): pl.pallas_call(rows_body, name='rows_pass', grid=(rows // (16 * ROW_GROUP...  7.23 us
  transfers between devices with their start and end apart: 8, of which 4 were waited for; matrix products, arithmetic and copies ran while one was open for 0% of the time, Pallas kernels for 1%

profile of v1, /device:TPU:21, one launch (start us, length us, event | category | flops | bytes accessed | tf_op | source)
XLA Modules:
  0.0 320.0 jit_solution(4970739231276016590)
XLA Ops:
  0.0 7.4 %pack.1 = (bf16[1024,2,16,128]{3,2,1,0:T(8,128)(2,1)}, s32[16,128]{1,0:T(8,128)S(1)}) custom-call(s32[1]{0:T(128)} %bitcast.mine_ref, bf16[2,1024,2048]{2,1,0:T(8,128)(2,1)} %x_ref.1, s32[1,128]{1,0:T(1,128)} %bitcast.6, s32[1,128]{1,0:T(1,128)} %bitcast.7, s32[1,128]{1,0:T(1,128)} %bitcast.8), custom_call_target="tpu_custom_call" | custom-call | tf_op jit(solution)/shard_map/pack/pallas_call | solution.py:114
  7.5 0.0 copy-start.1
  7.5 0.0 copy-start.3
  7.5 0.0 copy-start.4
  7.5 96.8 %all_to_all.10 = bf16[1024,2,16,128]{3,2,1,0:T(8,128)(2,1)S(1)} all-to-all(bf16[1024,2,16,128]{3,2,1,0:T(8,128)(2,1)} %get-tuple-element.17), channel_id=1, replica_groups=mesh['row'=16,'col'=8] {'col'}, dimensions={0} | all-to-all | bytes 16777216 | tf_op jit(solution)/shard_map/all_to_all | solution.py:356
  104.3 0.0 copy-done.3
  104.3 7.2 %rows_pass.1 = bf16[128,2,128,128]{3,2,1,0:T(8,128)(2,1)S(1)} custom-call(bf16[8,128,2,16,128]{4,3,2,1,0:T(8,128)(2,1)S(1)} %bitcast.5, bf16[256,256]{1,0:T(8,128)(2,1)S(1)} %copy-done.4, bf16[256,256]{1,0:T(8,128)(2,1)S(1)} %copy-done.1, f32[2,128,128]{2,1,0:T(8,128)S(1)} %copy-done.3), custom_call_target="tpu_custom_call" | custom-call | tf_op jit(solution)/shard_map/rows_pass/pallas_call | solution.py:170
  111.5 0.0 copy-start.2
  111.5 0.0 copy-start.5
  111.5 107.2 %all_to_all.11.x_ref = bf16[128,2,128,128]{3,2,1,0:T(8,128)(2,1)} all-to-all(bf16[128,2,128,128]{3,2,1,0:T(8,128)(2,1)S(1)} %rows_pass.1), channel_id=1, replica_groups=mesh['row'=16,'col'=8] {'row','col'}, dimensions={0} | all-to-all | bytes 16777216 | tf_op jit(solution)/shard_map/all_to_all | solution.py:359
  218.8 0.0 copy-done.2
  218.8 13.8 %columns_pass.1 = (bf16[2,1024,128]{2,1,0:T(8,128)(2,1)S(1)}, bf16[2,1024,128]{2,1,0:T(8,128)(2,1)S(1)}, bf16[2,1024,128]{2,1,0:T(8,128)(2,1)S(1)}, bf16[2,1024,...) custom-call(s32[16,128]{1,0:T(8,128)S(1)} %get-tuple-element.16.star, ...), custom_call_target="tpu_custom_call" | custom-call | tf_op jit(solution)/shard_map/columns_pass/pallas_call | solution.py:255
  232.6 1.9 collective-permute-start.4
  234.4 2.9 collective-permute-start.5
  237.4 2.5 collective-permute-start.6
  239.9 0.0 collective-permute-start
  239.9 1.5 collective-permute-start.7
  241.4 15.5 %collective-permute-done.4.refs_0_ = bf16[2,1024,128]{2,1,0:T(8,128)(2,1)S(1)} collective-permute-done((bf16[2,1024,128]{2,1,0:T(8,128)(2,1)S(1)}, bf16[2,1024,128]{2,1,0:T(8,128)(2,1)S(1)}, u32[]{:S(2)}, u32[]{:S(2)}) %collective-permute-start.4) | collective-permute-done | bytes 524320 | tf_op jit(solution)/shard_map/ppermute | solution.py:342
  256.9 23.5 %collective-permute-start.1 = (bf16[2,1024,128]{2,1,0:T(8,128)(2,1)S(1)}, bf16[2,1024,128]{2,1,0:T(8,128)(2,1)S(1)}, u32[]{:S(2)}, u32[]{:S(2)}) collective-permute-start(bf16[2,1024,128]{2,1,0:T(8,128)(2,1)S(1)} %get-tuple-element.20), channel_id=1, source_target_pairs={{2,0},{3,1},{4,2},{5,3},{6,4},{7,5},{8,6},{9,7},{10,8},{11,9},{12,... | collective-permute-start | bytes 1572872 | tf_op jit(solution)/shard_map/ppermute | solution.py:342
  280.4 0.0 collective-permute-done.5.refs_1_
  280.4 0.0 collective-permute-start.2
  280.4 0.0 collective-permute-done.6.refs_2_
  280.4 4.0 %collective-permute-start.3 = (bf16[2,1024,128]{2,1,0:T(8,128)(2,1)S(1)}, bf16[2,1024,128]{2,1,0:T(8,128)(2,1)S(1)}, u32[]{:S(2)}, u32[]{:S(2)}) collective-permute-start(bf16[2,1024,128]{2,1,0:T(8,128)(2,1)S(1)} %get-tuple-element.22), channel_id=1, source_target_pairs={{4,0},{5,1},{6,2},{7,3},{8,4},{9,5},{10,6},{11,7},{12,8},{13,9},{1... | collective-permute-start | bytes 1572872 | tf_op jit(solution)/shard_map/ppermute | solution.py:342
  284.4 0.0 collective-permute-done.7.refs_3_
  284.4 0.0 copy-done.6
  284.4 2.9 facet.2.refs_7_
  287.3 0.0 collective-permute-done.refs_1_
  287.3 6.1 %collective-permute-done.1.refs_2_ = bf16[2,1024,128]{2,1,0:T(8,128)(2,1)S(1)} collective-permute-done((bf16[2,1024,128]{2,1,0:T(8,128)(2,1)S(1)}, bf16[2,1024,128]{2,1,0:T(8,128)(2,1)S(1)}, u32[]{:S(2)}, u32[]{:S(2)}) %collective-permute-start.1) | collective-permute-done | bytes 524320 | tf_op jit(solution)/shard_map/ppermute | solution.py:342
  293.4 12.5 %collective-permute-done.2.refs_3_ = bf16[2,1024,128]{2,1,0:T(8,128)(2,1)S(1)} collective-permute-done((bf16[2,1024,128]{2,1,0:T(8,128)(2,1)S(1)}, bf16[2,1024,128]{2,1,0:T(8,128)(2,1)S(1)}, u32[]{:S(2)}, u32[]{:S(2)}) %collective-permute-start.2) | collective-permute-done | bytes 524320 | tf_op jit(solution)/shard_map/ppermute | solution.py:342
  305.9 11.2 %collective-permute-done.3.refs_4_ = bf16[2,1024,128]{2,1,0:T(8,128)(2,1)S(1)} collective-permute-done((bf16[2,1024,128]{2,1,0:T(8,128)(2,1)S(1)}, bf16[2,1024,128]{2,1,0:T(8,128)(2,1)S(1)}, u32[]{:S(2)}, u32[]{:S(2)}) %collective-permute-start.3) | collective-permute-done | bytes 524320 | tf_op jit(solution)/shard_map/ppermute | solution.py:342
  317.1 0.0 copy-done.7
  317.1 2.9 facet.3
  (7 shorter events, 0.0 us)
Async XLA Ops:
  7.5 96.8 %copy-start.1 = (bf16[256,256]{1,0:T(8,128)(2,1)S(1)}, bf16[256,256]{1,0:T(8,128)(2,1)}, u32[]{:S(2)}) copy-start(bf16[256,256]{1,0:T(8,128)(2,1)} %constant.28.clone.h_ref.f_ref) | copy-start | bytes 393220
  7.5 96.8 %copy-start.3 = (f32[2,128,128]{2,1,0:T(8,128)S(1)}, f32[2,128,128]{2,1,0:T(8,128)}, u32[]{:S(2)}) copy-start(f32[2,128,128]{2,1,0:T(8,128)} %constant.30.clone.tw_ref) | copy-start | bytes 393220
  7.5 96.8 %copy-start.4 = (bf16[256,256]{1,0:T(8,128)(2,1)S(1)}, bf16[256,256]{1,0:T(8,128)(2,1)}, u32[]{:S(2)}) copy-start(bf16[256,256]{1,0:T(8,128)(2,1)} %constant.27.clone.g_ref) | copy-start | bytes 393220
  111.5 107.2 %copy-start.2 = (f32[4,2,128,32]{3,2,1,0:T(8,128)S(1)}, f32[4,2,128,32]{3,2,1,0:T(8,128)}, u32[]{:S(2)}) copy-start(f32[4,2,128,32]{3,2,1,0:T(8,128)} %constant.31.clone.tw_ref) | copy-start | bytes 393220
  111.5 107.2 %copy-start.5 = (bf16[256,256]{1,0:T(8,128)(2,1)S(1)}, bf16[256,256]{1,0:T(8,128)(2,1)}, u32[]{:S(2)}) copy-start(bf16[256,256]{1,0:T(8,128)(2,1)} %constant.29.clone.g_ref) | copy-start | bytes 393220
  218.7 65.6 %copy-start = (f32[1024,1]{1,0:T(8,128)S(1)}, f32[1024,1]{1,0:T(8,128)}, u32[]{:S(2)}) copy-start(f32[1024,1]{1,0:T(8,128)} %constant.32.clone.refs_5_) | copy-start | bytes 12292
  218.8 65.6 %copy-start.6 = (f32[1,512]{1,0:T(1,128)S(1)}, f32[1,512]{1,0:T(1,128)}, u32[]{:S(2)}) copy-start(f32[1,512]{1,0:T(1,128)} %constant.33.clone.refs_6_) | copy-start | bytes 6148
  218.8 98.4 %copy-start.7 = (f32[1,512]{1,0:T(1,128)S(1)}, f32[1,512]{1,0:T(1,128)}, u32[]{:S(2)}) copy-start(f32[1,512]{1,0:T(1,128)} %constant.34.clone.refs_6_) | copy-start | bytes 6148
  232.6 24.3 %collective-permute-start.4 = (bf16[2,1024,128]{2,1,0:T(8,128)(2,1)S(1)}, bf16[2,1024,128]{2,1,0:T(8,128)(2,1)S(1)}, u32[]{:S(2)}, u32[]{:S(2)}) collective-permute-start(bf16[2,1024,128]{2,1,0:T(8,128)(2,1)S(1)} %get-tuple-element.23), channel_id=1, source_target_pairs={{124,0},{125,1},{126,2},{127,3},{0,4},{1,5},{2,6},{3,7},{4,8},{5,9... | collective-permute-start | bytes 1572872 | tf_op jit(solution)/shard_map/ppermute | solution.py:342
  234.4 45.9 %collective-permute-start.5 = (bf16[2,1024,128]{2,1,0:T(8,128)(2,1)S(1)}, bf16[2,1024,128]{2,1,0:T(8,128)(2,1)S(1)}, u32[]{:S(2)}, u32[]{:S(2)}) collective-permute-start(bf16[2,1024,128]{2,1,0:T(8,128)(2,1)S(1)} %get-tuple-element.24), channel_id=1, source_target_pairs={{125,0},{126,1},{127,2},{0,3},{1,4},{2,5},{3,6},{4,7},{5,8},{6,9},... | collective-permute-start | bytes 1572872 | tf_op jit(solution)/shard_map/ppermute | solution.py:342
  237.4 43.0 %collective-permute-start.6 = (bf16[2,1024,128]{2,1,0:T(8,128)(2,1)S(1)}, bf16[2,1024,128]{2,1,0:T(8,128)(2,1)S(1)}, u32[]{:S(2)}, u32[]{:S(2)}) collective-permute-start(bf16[2,1024,128]{2,1,0:T(8,128)(2,1)S(1)} %get-tuple-element.25), channel_id=1, source_target_pairs={{126,0},{127,1},{0,2},{1,3},{2,4},{3,5},{4,6},{5,7},{6,8},{7,9},{8... | collective-permute-start | bytes 1572872 | tf_op jit(solution)/shard_map/ppermute | solution.py:342
  239.9 47.4 %collective-permute-start = (bf16[2,1024,128]{2,1,0:T(8,128)(2,1)S(1)}, bf16[2,1024,128]{2,1,0:T(8,128)(2,1)S(1)}, u32[]{:S(2)}, u32[]{:S(2)}) collective-permute-start(bf16[2,1024,128]{2,1,0:T(8,128)(2,1)S(1)} %get-tuple-element.19), channel_id=1, source_target_pairs={{1,0},{2,1},{3,2},{4,3},{5,4},{6,5},{7,6},{8,7},{9,8},{10,9},{11,1... | collective-permute-start | bytes 1572872 | tf_op jit(solution)/shard_map/ppermute | solution.py:342
  239.9 44.5 %collective-permute-start.7 = (bf16[2,1024,128]{2,1,0:T(8,128)(2,1)S(1)}, bf16[2,1024,128]{2,1,0:T(8,128)(2,1)S(1)}, u32[]{:S(2)}, u32[]{:S(2)}) collective-permute-start(bf16[2,1024,128]{2,1,0:T(8,128)(2,1)S(1)} %get-tuple-element.26), channel_id=1, source_target_pairs={{127,0},{0,1},{1,2},{2,3},{3,4},{4,5},{5,6},{6,7},{7,8},{8,9},{9,1... | collective-permute-start | bytes 1572872 | tf_op jit(solution)/shard_map/ppermute | solution.py:342
  256.9 36.5 %collective-permute-start.1 = (bf16[2,1024,128]{2,1,0:T(8,128)(2,1)S(1)}, bf16[2,1024,128]{2,1,0:T(8,128)(2,1)S(1)}, u32[]{:S(2)}, u32[]{:S(2)}) collective-permute-start(bf16[2,1024,128]{2,1,0:T(8,128)(2,1)S(1)} %get-tuple-element.20), channel_id=1, source_target_pairs={{2,0},{3,1},{4,2},{5,3},{6,4},{7,5},{8,6},{9,7},{10,8},{11,9},{12,... | collective-permute-start | bytes 1572872 | tf_op jit(solution)/shard_map/ppermute | solution.py:342
  280.4 25.5 %collective-permute-start.2 = (bf16[2,1024,128]{2,1,0:T(8,128)(2,1)S(1)}, bf16[2,1024,128]{2,1,0:T(8,128)(2,1)S(1)}, u32[]{:S(2)}, u32[]{:S(2)}) collective-permute-start(bf16[2,1024,128]{2,1,0:T(8,128)(2,1)S(1)} %get-tuple-element.21), channel_id=1, source_target_pairs={{3,0},{4,1},{5,2},{6,3},{7,4},{8,5},{9,6},{10,7},{11,8},{12,9},{13... | collective-permute-start | bytes 1572872 | tf_op jit(solution)/shard_map/ppermute | solution.py:342
  280.4 36.8 %collective-permute-start.3 = (bf16[2,1024,128]{2,1,0:T(8,128)(2,1)S(1)}, bf16[2,1024,128]{2,1,0:T(8,128)(2,1)S(1)}, u32[]{:S(2)}, u32[]{:S(2)}) collective-permute-start(bf16[2,1024,128]{2,1,0:T(8,128)(2,1)S(1)} %get-tuple-element.22), channel_id=1, source_target_pairs={{4,0},{5,1},{6,2},{7,3},{8,4},{9,5},{10,6},{11,7},{12,8},{13,9},{1... | collective-permute-start | bytes 1572872 | tf_op jit(solution)/shard_map/ppermute | solution.py:342
